TPU v7x, 128 devices: a whole 4x4x4 slice. The times are simulated.
128 devices in a mesh: blk: 4 (over x), tok: 32 (over y, z, core).
Axes of the slice: x: 4, y: 4, z: 4, core: 2. Of those that a mesh axis runs over, the one named last changes fastest.
Arguments:
- tokens: bfloat16 [32, 1024, 1664], P('tok', 'blk'), may hold values from -6 to 6
- segment_ids: int32 [32, 1024], P('tok'), may hold values from 0 to 31, as said below
- merge_index: int32 [32, 256, 4], P('tok'), may hold values from 0 to 1023, as said below
- segment_owner: int32 [32, 32], P('tok'), may hold values from 0 to 31, each once within a row
- ln1_gain: float32 [1664], replicated, may hold values from 0.1 to 1.9
- ln1_bias: float32 [1664], replicated, may hold values from -4 to 4
- w_qkv: bfloat16 [3, 1664, 1664], P(None, 'tok', 'blk'), may hold values from -0.15625 to 0.15625
- qkv_bias: float32 [3, 1664], P(None, 'blk'), may hold values from -6 to 6
- w_out: bfloat16 [1664, 1664], P('blk', 'tok'), may hold values from -0.15625 to 0.15625
- out_bias: float32 [1664], replicated, may hold values from -6 to 6
- ln2_gain: float32 [1664], replicated, may hold values from 0.1 to 1.9
- ln2_bias: float32 [1664], replicated, may hold values from -4 to 4
- w_fc1: bfloat16 [1664, 8192], P(None, 'blk'), may hold values from -0.15625 to 0.15625
- fc1_bias: float32 [8192], P('blk'), may hold values from -6 to 6
- w_fc2: bfloat16 [8192, 1664], P('blk'), may hold values from -0.0625 to 0.0625
- fc2_bias: float32 [1664], replicated, may hold values from -6 to 6
- ln3_gain: float32 [1664], replicated, may hold values from 0.1 to 1.9
- ln3_bias: float32 [1664], replicated, may hold values from -4 to 4
- w_proj: bfloat16 [6656, 1664], P('tok', 'blk'), may hold values from -0.078125 to 0.078125
- proj_bias: float32 [1664], P('blk'), may hold values from -6 to 6
Outputs:
- returned: bfloat16 [32, 32, 16, 1664], P('tok', None, None, 'blk')
Inputs may be any that keep to these rules, and one draw needn't show every extreme that they name: `segment_ids`: within a block each segment holds 4 to 64 tokens, one exactly 64; the four tokens of one row of merge_index share a segment. `merge_index`: the rows of one block name each token of the block exactly once. `segment_owner`: each block's row is a permutation of the owners.
All inputs are finite; a program needn't handle non-finite values.
Results may differ from a plain program's by a relative error of at most 0.015.
Values may be sent and summed in bfloat16 or wider, within the bound.
A program may use at most 128 MiB of HBM per device.

v0:
```python
import math
import jax
import jax.numpy as jnp
from jax import lax
from jax.sharding import PartitionSpec as P

HD = 104
EPS = 1e-06


def layer_norm(input_tensors, scales, offset):
    input_tensors = input_tensors.astype(jnp.float32)
    center = input_tensors - jnp.mean(input_tensors, axis=-1, keepdims=True)
    spread = jnp.mean(center * center, axis=-1, keepdims=True)
    return center * lax.rsqrt(spread + EPS) * scales + offset


def body(
    tokens,
    segment_ids,
    merge_index,
    segment_owner,
    ln1_gain,
    ln1_bias,
    w_qkv,
    qkv_bias,
    w_out,
    out_bias,
    ln2_gain,
    ln2_bias,
    w_fc1,
    fc1_bias,
    w_fc2,
    fc2_bias,
    ln3_gain,
    ln3_bias,
    w_proj,
    proj_bias,
):
    tok_block = tokens[0]
    row_count = tok_block.shape[0]
    model_width = tok_block.shape[1]
    head_cols = w_qkv.shape[2]
    heads_here = head_cols // HD
    normed_one = layer_norm(tok_block, ln1_gain, ln1_bias).astype(jnp.bfloat16)
    normed_all = lax.all_gather(normed_one, "blk", axis=0, tiled=True)
    all_rows = normed_all.shape[0]
    columns = normed_all
    projected_qkv = jnp.einsum(
        "td,cde->cte",
        columns,
        lax.all_gather(w_qkv, "tok", axis=1, tiled=True),
        preferred_element_type=jnp.float32,
    )
    projected_qkv = (projected_qkv + qkv_bias[:, None, :]).astype(jnp.bfloat16)
    projected_qkv = projected_qkv.reshape(3, all_rows, heads_here, HD)
    key_rows = projected_qkv[1]
    values = projected_qkv[2]
    segment_row = segment_ids[0]
    q_block = min(512, all_rows)
    block_count = all_rows // q_block
    query_rows = projected_qkv[0].reshape(block_count, q_block, heads_here, HD)
    query_segs = segment_row.reshape(block_count, q_block)
    score_scale = 1.0 / math.sqrt(HD)

    def attend(input_tensors):
        query_part, query_seg = input_tensors
        scores = (
            jnp.einsum("qhe,khe->hqk", query_part, key_rows, preferred_element_type=jnp.float32)
            * score_scale
        )
        allowed = query_seg[:, None] == segment_row[None, :]
        weights = jnp.where(allowed[None], jnp.exp(scores), 0.0)
        attn_probs = (weights / jnp.sum(weights, axis=-1, keepdims=True)).astype(jnp.bfloat16)
        mixed = jnp.einsum("hqk,khe->qhe", attn_probs, values, preferred_element_type=jnp.float32)
        return mixed.astype(jnp.bfloat16)

    attended = lax.map(attend, (query_rows, query_segs)).reshape(all_rows, head_cols)
    out_full = lax.all_gather(w_out, "tok", axis=1, tiled=True)
    attn_rows = lax.psum_scatter(
        jnp.dot(attended, out_full, preferred_element_type=jnp.float32).astype(jnp.bfloat16),
        "blk",
        scatter_dimension=0,
        tiled=True,
    ).astype(jnp.float32)
    after_attn = tok_block.astype(jnp.float32) + attn_rows + out_bias
    normed_two = layer_norm(after_attn, ln2_gain, ln2_bias).astype(jnp.bfloat16)
    pre_act = (
        jnp.dot(
            lax.all_gather(normed_two, "blk", axis=0, tiled=True),
            w_fc1,
            preferred_element_type=jnp.float32,
        )
        + fc1_bias
    )
    hidden_act = jax.nn.gelu(pre_act, approximate=False).astype(jnp.bfloat16)
    partial_sum = jnp.dot(hidden_act, w_fc2, preferred_element_type=jnp.float32)
    own_start = lax.axis_index("blk") * row_count
    own_rows = lax.dynamic_slice_in_dim(partial_sum, own_start, row_count, 0) + after_attn
    partial_sum = lax.dynamic_update_slice_in_dim(partial_sum, own_rows, own_start, 0)
    summed = lax.psum(partial_sum.astype(jnp.bfloat16), "blk").astype(jnp.float32)
    layer_all = (summed + fc2_bias).astype(jnp.bfloat16)
    final_all = layer_norm(layer_all, ln3_gain, ln3_bias).astype(jnp.bfloat16)
    merge_rows = merge_index[0]
    merged_count = merge_rows.shape[0]
    merged = jnp.take(final_all, merge_rows.reshape(-1), axis=0).reshape(
        merged_count, 4 * model_width
    )
    columns = merged
    projected = jnp.dot(
        columns,
        lax.all_gather(w_proj, "tok", axis=0, tiled=True),
        preferred_element_type=jnp.float32,
    )
    projected = (projected + proj_bias).astype(jnp.bfloat16)
    tok_count = lax.axis_size("tok")
    slot_cap = 2 * merged_count // tok_count
    owners_here = segment_owner[0]
    seg_rows = jnp.take(segment_row, merge_rows[:, 0])
    seg_match = (
        seg_rows[:, None] == jnp.arange(owners_here.shape[0], dtype=jnp.int32)[None, :]
    ).astype(jnp.int32)
    owner_rows = jnp.sum(seg_match * owners_here[None, :], axis=1)
    segment_matches = (
        owner_rows[:, None] == jnp.arange(tok_count, dtype=jnp.int32)[None, :]
    ).astype(jnp.int32)
    before = jnp.cumsum(segment_matches, axis=0) - segment_matches
    order_in = jnp.sum(before * segment_matches, axis=1)
    target = owner_rows * slot_cap + order_in
    placed = (jnp.arange(tok_count * slot_cap, dtype=jnp.int32)[:, None] == target[None, :]).astype(
        jnp.bfloat16
    )
    outgoing = jnp.dot(placed, projected, preferred_element_type=jnp.float32).astype(jnp.bfloat16)
    outgoing = outgoing.reshape(tok_count, slot_cap, projected.shape[1])
    arrived = lax.all_to_all(outgoing, "tok", split_axis=0, concat_axis=0, tiled=True)
    return arrived[None]


def solution(mesh):
    placed = (
        P("tok", "blk", None),
        P("tok", None),
        P("tok", None, None),
        P("tok", None),
        P(),
        P(),
        P(None, "tok", "blk"),
        P(None, "blk"),
        P("blk", "tok"),
        P(),
        P(),
        P(),
        P(None, "blk"),
        P("blk"),
        P("blk", None),
        P(),
        P(),
        P(),
        P("tok", "blk"),
        P("blk"),
    )
    return jax.shard_map(
        body, mesh=mesh, in_specs=placed, out_specs=P("tok", None, None, "blk"), check_vma=False
    )
```

profile of v0, /device:TPU:1, one launch (start us, length us, event | category | flops | bytes accessed | tf_op | source)
XLA Modules:
  0.0 480.8 jit_solution(5821261523930769322)
XLA Ops:
  6.5 0.7 all-gather.15.cloned.1.call-update
  7.3 0.0 all-gather.7.cloned.1.call-start
  7.3 1.3 convert_reduce_fusion.1
  8.7 1.5 fusion.43
  10.2 2.5 fusion.46
  12.8 0.0 all-gather.9.cloned.1.call-start
  12.8 1.7 copy.32
  14.5 0.0 reduce-scatter.2.cloned.1.call-start
  14.6 0.5 broadcast.197
  15.1 1.3 reduce.6
  16.4 40.5 %all-gather.15.cloned.1.call-done = bf16[32,52,416]{2,1,0:T(8,128)(2,1)} async-done(((bf16[1,52,416]{2,1,0:T(8,128)(2,1)}), bf16[32,52,416]{2,1,0:T(8,128)(2,1)}) %all-gather.15.cloned.1.call-update) | async-done | bytes 1384464 | tf_op jit(solution)/shard_map/all_gather | solution.py:79
  56.9 2.7 reshape.179
  59.7 39.4 %all-gather.7.cloned.1.call-done = bf16[1024,1664]{1,0:T(8,128)(2,1)} async-done(((bf16[256,1664]{1,0:T(8,128)(2,1)}), bf16[1024,1664]{1,0:T(8,128)(2,1)}) %all-gather.7.cloned.1.call-update) | async-done | bytes 3407888 | tf_op jit(solution)/shard_map/all_gather | solution.py:46
  99.1 53.1 %all-gather.9.cloned.1.call-done = bf16[3,1664,416]{2,0,1:T(4,128)(2,1)} async-done(((bf16[3,52,416]{2,0,1:T(4,128)(2,1)}), bf16[3,1664,416]{2,0,1:T(4,128)(2,1)}) %all-gather.9.cloned.1.call-update) | async-done | bytes 4153360 | tf_op jit(solution)/shard_map/all_gather | solution.py:52
  152.2 9.2 %fusion.34 = bf16[3,1024,416]{1,2,0:T(8,128)(2,1)S(1)} fusion(f32[3,416]{1,0:T(4,128)S(1)} %copy-done.15, bf16[3,1664,416]{2,0,1:T(4,128)(2,1)} %all-gather.9.cloned.1.call-done, bf16[1024,1664]{1,0:T(8,128)(2,1)} %all-gather.7.cloned.1.call-done), kind=kOutput, calls=%fused_computation.53 | convolution fusion | flops 4255580160 | bytes 10122112 | tf_op jit(solution)/shard_map/td,cde->cte/dot_general | solution.py:49
  161.4 1.4 fusion.96
  162.8 0.6 reshape_squeeze.10
  163.4 1.0 copy.34
  164.4 15.8 %while.10 = (s32[]{:T(128)}, bf16[2,512,4,104]{1,3,2,0:T(8,128)(2,1)}, s32[2,512]{1,0:T(2,128)S(1)}, s32[1,1024]{1,0:T(1,128)S(1)}, bf16[2,512,4,104]{1,3,2,0:T(...) while((s32[]{:T(128)}, bf16[2,512,4,104]{1,3,2,0:T(8,128)(2,1)}, ...), condition=%wide.region_8.9_spmd, body=%wide.region_6.8_spmd.sunk | while | flops 887830528 | bytes 31156912 | solution.py:78
  164.4 0.4 broadcast_compare_fusion.2
  164.8 4.0 fusion.112
  168.8 2.5 fusion.113
  171.3 0.9 copy-done.6
  172.3 0.4 broadcast_compare_fusion.2
  172.6 4.0 fusion.112
  176.6 2.5 fusion.113
  179.2 0.9 copy-done.6
  180.2 2.0 copy.35
  182.2 0.2 copy.40
  182.4 3.9 convolution_convert_fusion
  186.4 0.0 all-gather.11.cloned.1.call-start
  186.4 38.9 %reduce-scatter.2.cloned.1.call-done = bf16[256,1664]{1,0:T(8,128)(2,1)} async-done(((bf16[1024,1664]{1,0:T(8,128)(2,1)}), bf16[256,1664]{1,0:T(8,128)(2,1)}) %reduce-scatter.2.cloned.1.call-update) | async-done | bytes 851984 | tf_op jit(solution)/shard_map/reduce_scatter | solution.py:80
  225.3 1.5 fusion.57
  226.9 1.7 multiply_reduce_fusion
  228.5 2.6 add_convert_fusion.2
  231.2 0.0 all-reduce.2.cloned.1.call-start
  231.3 41.5 %all-gather.11.cloned.1.call-done = bf16[1024,1664]{1,0:T(8,128)(2,1)} async-done(((bf16[256,1664]{1,0:T(8,128)(2,1)}), bf16[1024,1664]{1,0:T(8,128)(2,1)}) %all-gather.11.cloned.1.call-update) | async-done | bytes 3407888 | tf_op jit(solution)/shard_map/all_gather | solution.py:90
  272.7 11.1 %fusion.97 = f32[1024,2048]{1,0:T(8,128)S(1)} fusion(bf16[1024,1664]{1,0:T(8,128)(2,1)} %all-gather.11.cloned.1.call-done, bf16[1664,2048]{1,0:T(8,128)(2,1)} %param.34), kind=kOutput, calls=%fused_computation.133 | convolution fusion | flops 6979321856 | bytes 18612224 | tf_op jit(solution)/shard_map/dot_general | solution.py:89
  283.9 28.8 %fusion.29 = f32[1024,1664]{1,0:T(8,128)S(1)} fusion(bf16[2048,1664]{1,0:T(8,128)(2,1)} %param.36, f32[1024,2048]{1,0:T(8,128)S(1)} %fusion.97, f32[2048]{0:T(1024)S(1)} %copy-done.16), kind=kOutput, calls=%fused_computation.48 | convolution fusion | flops 7117733888 | bytes 22028288 | tf_op jit(solution)/shard_map/dot_general | solution.py:97
  312.8 0.4 add_dynamic-update-slice_fusion
  313.2 2.2 convert_element_type.78
  315.4 0.0 all-gather.13.cloned.1.call-start
  315.5 0.7 all-gather.13.cloned.1.call-update
  316.2 0.1 copy.36
  316.4 0.1 reshape_squeeze.11
  316.5 1.4 gather_fusion
  317.9 0.1 select_reduce_fusion
  318.0 0.6 reduce-window.6
  318.6 0.2 slice_reduce_fusion
  318.8 0.2 copy.31
  319.0 0.9 broadcast_in_dim.40
  320.0 2.0 copy.39
  322.0 0.1 fusion.62
  322.1 73.7 %all-reduce.2.cloned.1.call-done = bf16[1024,1664]{1,0:T(8,128)(2,1)} async-done(((bf16[1024,1664]{1,0:T(8,128)(2,1)}), bf16[1024,1664]{1,0:T(8,128)(2,1)}) %all-reduce.2.cloned.1.call-update) | async-done | bytes 3407888 | tf_op jit(solution)/shard_map/psum | solution.py:101
  395.8 2.8 convert_reduce_fusion
  398.7 3.2 fusion.23
  401.9 1.8 fusion.26
  403.7 5.9 %gather_fusion.1 = bf16[1024,1664]{1,0:T(8,128)(2,1)} fusion(bf16[1024,1664]{1,0:T(8,128)(2,1)S(1)} %fusion.26, s32[1024]{0:T(1024)S(1)} %broadcast_clamp_fusion), kind=kCustom, calls=%fused_computation.1 | custom fusion | bytes 6819840 | tf_op jit(solution)/shard_map/jit(_take)/gather | solution.py:106
  409.6 5.4 %gather.15 = bf16[256,6656]{1,0:T(8,128)(2,1)S(1)} reshape(bf16[1024,1664]{1,0:T(8,128)(2,1)} %gather_fusion.1) | data formatting | bytes 6815744 | tf_op jit(solution)/shard_map/jit(_take)/gather | solution.py:106
  415.0 33.5 %all-gather.13.cloned.1.call-done = bf16[6656,416]{1,0:T(8,128)(2,1)} async-done(((bf16[208,416]{1,0:T(8,128)(2,1)}), bf16[6656,416]{1,0:T(8,128)(2,1)}) %all-gather.13.cloned.1.call-update) | async-done | bytes 5537808 | tf_op jit(solution)/shard_map/all_gather | solution.py:112
  448.5 7.0 %convolution_convert_fusion.1 = bf16[512,416]{0,1:T(8,128)(2,1)} fusion(bf16[6656,416]{1,0:T(8,128)(2,1)} %all-gather.13.cloned.1.call-done, pred[256,6656]{1,0:T(8,128)(4,1)} %bitcast.118, bf16[256,6656]{1,0:T(8,128)(2,1)S(1)} %gather.15, s32[256]{0:T(256)S(1)} %multiply_add_fusion, f32[416]{0:T(512)S(1)} %copy-done.17), kind=kOutput, calls=%fused_computation.69 | convolution fusion | flops 1528987648 | bytes 11078272 | tf_op jit(solution)/shard_map/dot_general | solution.py:133
  455.5 1.2 copy.37
  456.7 16.2 %all_to_all.5 = bf16[32,16,416]{2,1,0:T(8,128)(2,1)S(1)} all-to-all(bf16[32,16,416]{2,1,0:T(8,128)(2,1)S(1)} %bitcast.116), channel_id=1, replica_groups=mesh['blk'=4,'tok'=32] {'tok'}, dimensions={0} | all-to-all | bytes 851968 | tf_op jit(solution)/shard_map/all_to_all | solution.py:135
  472.9 0.8 copy.56
  (66 shorter events, 0.3 us)
Async XLA Ops:
  6.5 145.7 %copy-start.15 = (f32[3,416]{1,0:T(4,128)S(1)}, f32[3,416]{1,0:T(4,128)}, u32[]{:S(2)}) copy-start(f32[3,416]{1,0:T(4,128)} %param.29) | copy-start | bytes 14980
  6.5 50.4 %all-gather.15.cloned.1.call-start = ((), (), s32[]{:S(2)}) async-start(), calls=%async_computation.8 | async-start | bytes 1892352 | tf_op jit(solution)/shard_map/all_gather | solution.py:79
  7.3 91.8 %all-gather.7.cloned.1.call-start = ((), (), s32[]{:S(2)}) async-start(), calls=%async_computation.2 | async-start | bytes 4259840 | tf_op jit(solution)/shard_map/all_gather | solution.py:46
  12.8 139.4 %all-gather.9.cloned.1.call-start = ((), (), s32[]{:S(2)}) async-start(), calls=%async_computation.3 | async-start | bytes 7028736 | tf_op jit(solution)/shard_map/all_gather | solution.py:52
  14.5 210.8 %reduce-scatter.2.cloned.1.call-start = ((), (), s32[]{:S(2)}) async-start(), calls=%async_computation.4 | async-start | bytes 4259840 | tf_op jit(solution)/shard_map/reduce_scatter | solution.py:80
  161.4 3.0 copy-start
  164.4 4.3 copy-start.4
  164.4 4.3 copy-start.5
  171.3 0.9 copy-start.6
  172.2 4.3 copy-start.4
  172.2 4.3 copy-start.5
  179.1 0.9 copy-start.6
  182.4 42.9 %copy-start.1 = (bf16[1,256,1664]{2,1,0:T(8,128)(2,1)S(1)}, bf16[1,256,1664]{2,1,0:T(8,128)(2,1)}, u32[]{:S(2)}) copy-start(bf16[1,256,1664]{2,1,0:T(8,128)(2,1)} %param.22) | copy-start | bytes 2555908
  182.4 42.9 %copy-start.7 = (f32[1664]{0:T(1024)S(1)}, f32[1664]{0:T(1024)}, u32[]{:S(2)}) copy-start(f32[1664]{0:T(1024)} %param.31) | copy-start | bytes 19972
  186.4 42.2 %copy-start.10 = (f32[1664]{0:T(1024)S(1)}, f32[1664]{0:T(1024)}, u32[]{:S(2)}) copy-start(f32[1664]{0:T(1024)} %param.33) | copy-start | bytes 19972
  186.4 42.2 %copy-start.11 = (f32[1664]{0:T(1024)S(1)}, f32[1664]{0:T(1024)}, u32[]{:S(2)}) copy-start(f32[1664]{0:T(1024)} %param.32) | copy-start | bytes 19972
  186.4 86.3 %all-gather.11.cloned.1.call-start = ((), (), s32[]{:S(2)}) async-start(), calls=%async_computation.5 | async-start | bytes 4259840 | tf_op jit(solution)/shard_map/all_gather | solution.py:90
  231.2 164.6 %all-reduce.2.cloned.1.call-start = ((), (), s32[]{:S(2)}) async-start(), calls=%async_computation.6 | async-start | bytes 6815744 | tf_op jit(solution)/shard_map/psum | solution.py:101
  231.2 52.6 %copy-start.16 = (f32[2048]{0:T(1024)S(1)}, f32[2048]{0:T(1024)}, u32[]{:S(2)}) copy-start(f32[2048]{0:T(1024)} %param.35) | copy-start | bytes 24580
  283.9 28.9 %copy-start.3 = (bf16[256,1664]{1,0:T(8,128)(2,1)S(1)}, bf16[256,1664]{1,0:T(8,128)(2,1)}, u32[]{:S(2)}) copy-start(bf16[256,1664]{1,0:T(8,128)(2,1)} %reduce-scatter.2.cloned.1.call-done) | copy-start | bytes 2555908
  313.2 3.0 copy-start.9
  313.2 4.7 copy-start.14
  315.4 80.4 %copy-start.8 = (f32[1664]{0:T(1024)S(1)}, f32[1664]{0:T(1024)}, u32[]{:S(2)}) copy-start(f32[1664]{0:T(1024)} %param.37) | copy-start | bytes 19972
  315.4 133.1 %all-gather.13.cloned.1.call-start = ((), (), s32[]{:S(2)}) async-start(), calls=%async_computation.7 | async-start | bytes 7028736 | tf_op jit(solution)/shard_map/all_gather | solution.py:112
  316.2 85.7 %copy-start.12 = (f32[1664]{0:T(1024)S(1)}, f32[1664]{0:T(1024)}, u32[]{:S(2)}) copy-start(f32[1664]{0:T(1024)} %param.39) | copy-start | bytes 19972
  316.2 85.6 %copy-start.13 = (f32[1664]{0:T(1024)S(1)}, f32[1664]{0:T(1024)}, u32[]{:S(2)}) copy-start(f32[1664]{0:T(1024)} %param.38) | copy-start | bytes 19972
  395.8 6.1 %copy-start.2 = (bf16[1024,1664]{1,0:T(8,128)(2,1)S(1)}, bf16[1024,1664]{1,0:T(8,128)(2,1)}, u32[]{:S(2)}) copy-start(bf16[1024,1664]{1,0:T(8,128)(2,1)} %all-reduce.2.cloned.1.call-done) | copy-start | bytes 10223620
  409.6 39.0 %copy-start.17 = (f32[416]{0:T(512)S(1)}, f32[416]{0:T(512)}, u32[]{:S(2)}) copy-start(f32[416]{0:T(512)} %param.41) | copy-start | bytes 4996
Sparse Core Ops, SparseCore 0:
  9.6 47.2 all-gather.14
  58.6 40.4 all-gather.6
  101.3 50.8 all-gather.8
  186.5 38.7 reduce-scatter.1
  231.3 41.3 all-gather.10
  315.5 80.1 all-reduce.1
  398.0 50.4 all-gather.12
where the time goes:
time: 490 us; the launch traced here: 481 us
  waiting for transfers between devices  322 us (66%)
  matrix products  73 us (15%)
  local copies, waits for them, and re-layouts  30.3 us (6%)
  other arithmetic  24.6 us (5%)
  blocking collectives  16.2 us (3%)
  between operations  14 us (3%)
    psum x1, waiting for transfers between devices, body(): lax.psum(partial_sum.astype(jnp.bfloat16), 'blk').astype(jnp.float32)  73.7 us
    all_gather x1, waiting for transfers between devices, body(): lax.all_gather(w_qkv, 'tok', axis=1, tiled=True)  53.1 us
    all_gather x1, waiting for transfers between devices, body(): lax.all_gather(normed_two, 'blk', axis=0, tiled=True)  41.5 us
    all_gather x1, waiting for transfers between devices, body(): out_full = lax.all_gather(w_out, 'tok', axis=1, tiled=True)  40.5 us
    all_gather x1, waiting for transfers between devices, body(): normed_all = lax.all_gather(normed_one, 'blk', axis=0, tiled=True)  39.4 us
    reduce_scatter x1, waiting for transfers between devices, body(): lax.psum_scatter(jnp.dot(attended, out_full, preferred_element_type=jnp.f...  38.9 us
    all_gather x1, waiting for transfers between devices, body(): lax.all_gather(w_proj, 'tok', axis=0, tiled=True)  33.5 us
    dot_general x1, matrix products, body(): partial_sum = jnp.dot(hidden_act, w_fc2, preferred_element_type=jnp.float32)  28.8 us
  transfers between devices with their start and end apart: 7, of which 7 were waited for; matrix products, arithmetic and copies ran while one was open for 8% of the time, Pallas kernels for 0%

commit v1 on v0

--- a/solution.py
+++ b/solution.py
@@ -43,7 +43,12 @@
     head_cols = w_qkv.shape[2]
     heads_here = head_cols // HD
     normed_one = layer_norm(tok_block, ln1_gain, ln1_bias).astype(jnp.bfloat16)
-    normed_all = lax.all_gather(normed_one, "blk", axis=0, tiled=True)
+    ring = [normed_one]
+    for hop in range(3):
+        ring.append(lax.ppermute(ring[-1], "blk", [(dev, (dev + 1) % 4) for dev in range(4)]))
+    normed_all = jnp.roll(
+        jnp.concatenate(ring[::-1], axis=0), (lax.axis_index("blk") + 1) * ring[0].shape[0], axis=0
+    )
     all_rows = normed_all.shape[0]
     columns = normed_all
     projected_qkv = jnp.einsum(

time: 490 us -> 439 us (0.90); the launches traced: 481 us -> 436 us
  waiting for transfers between devices: 322 us -> 267 us
  local copies, waits for them, and re-layouts: 30.3 us -> 35.3 us
    ppermute x0 -> x3, waiting for transfers between devices: none -> 56.7 us  [body(): lax.ppermute(ring[-1], 'blk', [(dev, (dev + 1) % 4) for dev in range(4)])]
    all_gather x1, waiting for transfers between devices: 40.5 us -> 0.01 us  [body(): out_full = lax.all_gather(w_out, 'tok', axis=1, tiled=True)]
    all_gather x1 -> x0, waiting for transfers between devices: 39.4 us -> none  [body(): normed_all = lax.all_gather(normed_one, 'blk', axis=0, tiled=True)]
    all_gather x1, waiting for transfers between devices: 53.1 us -> 21.4 us  [body(): lax.all_gather(w_qkv, 'tok', axis=1, tiled=True)]
    unnamed x37 -> x49, local copies, waits for them, and re-layouts: 8.1 us -> 15.2 us
  transfers between devices with their start and end apart: 7 -> 9, of which waited for: 7 -> 8; matrix products, arithmetic and copies ran while one was open for 8% -> 10% of each run, Pallas kernels for 0% -> 0%
where the time goes in v1:
time: 439 us; the launch traced here: 436 us
  waiting for transfers between devices  267 us (61%)
  matrix products  74.3 us (17%)
  local copies, waits for them, and re-layouts  35.3 us (8%)
  other arithmetic  26.3 us (6%)
  blocking collectives  16.2 us (4%)
  between operations  14.1 us (3%)
    psum x1, waiting for transfers between devices, body(): lax.psum(partial_sum.astype(jnp.bfloat16), 'blk').astype(jnp.float32)  73.9 us
    ppermute x3, waiting for transfers between devices, body(): lax.ppermute(ring[-1], 'blk', [(dev, (dev + 1) % 4) for dev in range(4)])  56.7 us
    all_gather x1, waiting for transfers between devices, body(): lax.all_gather(normed_two, 'blk', axis=0, tiled=True)  41.5 us
    reduce_scatter x1, waiting for transfers between devices, body(): lax.psum_scatter(jnp.dot(attended, out_full, preferred_element_type=jnp.f...  38.9 us
    all_gather x1, waiting for transfers between devices, body(): lax.all_gather(w_proj, 'tok', axis=0, tiled=True)  33.4 us
    dot_general x1, matrix products, body(): partial_sum = jnp.dot(hidden_act, w_fc2, preferred_element_type=jnp.float32)  28.6 us
    all_gather x1, waiting for transfers between devices, body(): lax.all_gather(w_qkv, 'tok', axis=1, tiled=True)  21.4 us
    all_to_all x1, blocking collectives, body(): lax.all_to_all(outgoing, 'tok', split_axis=0, concat_axis=0, tiled=True)  16.2 us
  transfers between devices with their start and end apart: 9, of which 8 were waited for; matrix products, arithmetic and copies ran while one was open for 10% of the time, Pallas kernels for 0%

profile of v1, /device:TPU:1, one launch (start us, length us, event | category | flops | bytes accessed | tf_op | source)
XLA Modules:
  0.0 436.2 jit_solution(14914839660769495858)
XLA Ops:
  6.5 0.7 all-gather.12.cloned.1.call-update
  7.3 1.7 copy.32
  9.1 1.3 convert_reduce_fusion.1
  10.5 1.5 fusion.44
  12.0 1.6 fusion.47
  13.6 2.1 collective-permute-start
  15.7 19.6 %collective-permute-done = bf16[256,1664]{1,0:T(8,128)(2,1)S(1)} collective-permute-done((bf16[256,1664]{1,0:T(8,128)(2,1)S(1)}, bf16[256,1664]{1,0:T(8,128)(2,1)S(1)}, u32[]{:S(2)}, u32[]{:S(2)}) %collective-permute-start) | collective-permute-done | bytes 852000 | tf_op jit(solution)/shard_map/ppermute | solution.py:48
  35.3 0.3 collective-permute-start.1
  35.6 19.8 %collective-permute-done.1 = bf16[256,1664]{1,0:T(8,128)(2,1)S(1)} collective-permute-done((bf16[256,1664]{1,0:T(8,128)(2,1)S(1)}, bf16[256,1664]{1,0:T(8,128)(2,1)S(1)}, u32[]{:S(2)}, u32[]{:S(2)}) %collective-permute-start.1) | collective-permute-done | bytes 852000 | tf_op jit(solution)/shard_map/ppermute | solution.py:48
  55.4 0.2 collective-permute-start.2
  55.6 0.5 broadcast.198
  56.1 1.3 reduce.6
  57.4 17.3 %collective-permute-done.2 = bf16[256,1664]{1,0:T(8,128)(2,1)S(1)} collective-permute-done((bf16[256,1664]{1,0:T(8,128)(2,1)S(1)}, bf16[256,1664]{1,0:T(8,128)(2,1)S(1)}, u32[]{:S(2)}, u32[]{:S(2)}) %collective-permute-start.2) | collective-permute-done | bytes 852000 | tf_op jit(solution)/shard_map/ppermute | solution.py:48
  74.7 1.0 constant_dynamic-update-slice_fusion.7
  75.6 1.0 constant_dynamic-update-slice_fusion.6
  76.7 1.0 constant_dynamic-update-slice_fusion.5
  77.7 1.3 constant_dynamic-update-slice_fusion.4
  79.0 1.0 constant_dynamic-update-slice_fusion.3
  80.0 1.0 constant_dynamic-update-slice_fusion.2
  80.9 1.0 constant_dynamic-update-slice_fusion.1
  81.9 1.4 constant_dynamic-update-slice_fusion
  83.3 3.9 reshape.179
  87.2 21.4 %all-gather.6.cloned.1.call-done = bf16[3,1664,416]{2,0,1:T(4,128)(2,1)} async-done(((bf16[3,52,416]{2,0,1:T(4,128)(2,1)}), bf16[3,1664,416]{2,0,1:T(4,128)(2,1)}) %all-gather.6.cloned.1.call-update) | async-done | bytes 4153360 | tf_op jit(solution)/shard_map/all_gather | solution.py:57
  108.6 9.2 %fusion.35 = bf16[3,1024,416]{1,2,0:T(8,128)(2,1)S(1)} fusion(f32[3,416]{1,0:T(4,128)S(1)} %copy-done.15, bf16[3,1664,416]{2,0,1:T(4,128)(2,1)} %all-gather.6.cloned.1.call-done, bf16[2048,1664]{1,0:T(8,128)(2,1)} %constant_dynamic-update-slice_fusion, s32[]{:T(128)S(6)} %select_n.59), kind=kOutput, calls=%fused_computation.54 | convolution fusion | flops 4255580160 | bytes 12784516 | tf_op jit(solution)/shard_map/td,cde->cte/dot_general | solution.py:54
  117.8 1.1 fusion.98
  118.9 0.6 reshape_squeeze.10
  119.5 1.0 copy.34
  120.5 15.2 %while.10 = (s32[]{:T(128)}, bf16[2,512,4,104]{1,3,2,0:T(8,128)(2,1)}, s32[2,512]{1,0:T(2,128)S(1)}, s32[1,1024]{1,0:T(1,128)S(1)}, bf16[2,512,4,104]{1,3,2,0:T(...) while((s32[]{:T(128)}, bf16[2,512,4,104]{1,3,2,0:T(8,128)(2,1)}, ...), condition=%wide.region_8.9_spmd, body=%wide.region_6.8_spmd.sunk | while | flops 887830528 | bytes 20933720 | solution.py:83
  120.6 0.4 broadcast_compare_fusion.2
  120.9 4.0 fusion.114
  124.9 3.2 fusion.115
  128.1 0.4 broadcast_compare_fusion.2
  128.5 3.8 fusion.114
  132.3 3.2 fusion.115
  135.7 2.0 copy.35
  137.8 0.2 copy.40
  138.0 3.9 convolution_convert_fusion
  142.0 38.9 %reduce-scatter.2.cloned.1.call-done = bf16[256,1664]{1,0:T(8,128)(2,1)} async-done(((bf16[1024,1664]{1,0:T(8,128)(2,1)}), bf16[256,1664]{1,0:T(8,128)(2,1)}) %reduce-scatter.2.cloned.1.call-update) | async-done | bytes 851984 | tf_op jit(solution)/shard_map/reduce_scatter | solution.py:85
  180.9 1.5 fusion.58
  182.4 1.7 multiply_reduce_fusion
  184.1 2.6 add_convert_fusion.2
  186.8 41.5 %all-gather.8.cloned.1.call-done = bf16[1024,1664]{1,0:T(8,128)(2,1)} async-done(((bf16[256,1664]{1,0:T(8,128)(2,1)}), bf16[1024,1664]{1,0:T(8,128)(2,1)}) %all-gather.8.cloned.1.call-update) | async-done | bytes 3407888 | tf_op jit(solution)/shard_map/all_gather | solution.py:95
  228.3 11.3 %fusion.99 = f32[1024,2048]{1,0:T(8,128)S(1)} fusion(bf16[1024,1664]{1,0:T(8,128)(2,1)} %all-gather.8.cloned.1.call-done, bf16[1664,2048]{1,0:T(8,128)(2,1)} %param.34), kind=kOutput, calls=%fused_computation.143 | convolution fusion | flops 6979321856 | bytes 18612224 | tf_op jit(solution)/shard_map/dot_general | solution.py:94
  239.6 28.6 %fusion.29 = f32[1024,1664]{1,0:T(8,128)S(1)} fusion(bf16[2048,1664]{1,0:T(8,128)(2,1)} %param.36, f32[1024,2048]{1,0:T(8,128)S(1)} %fusion.99, f32[2048]{0:T(1024)S(1)} %copy-done.16), kind=kOutput, calls=%fused_computation.48 | convolution fusion | flops 7117733888 | bytes 22028288 | tf_op jit(solution)/shard_map/dot_general | solution.py:102
  268.3 0.4 add_dynamic-update-slice_fusion
  268.8 2.2 convert_element_type.78
  271.0 0.5 all-gather.10.cloned.1.call-update
  271.9 1.4 gather_fusion
  273.4 0.6 reduce-window.6
  274.0 0.2 slice_reduce_fusion
  274.2 0.2 copy.31
  274.4 0.9 broadcast_in_dim.40
  275.4 2.0 copy.39
  277.5 73.9 %all-reduce.2.cloned.1.call-done = bf16[1024,1664]{1,0:T(8,128)(2,1)} async-done(((bf16[1024,1664]{1,0:T(8,128)(2,1)}), bf16[1024,1664]{1,0:T(8,128)(2,1)}) %all-reduce.2.cloned.1.call-update) | async-done | bytes 3407888 | tf_op jit(solution)/shard_map/psum | solution.py:106
  351.3 2.8 convert_reduce_fusion
  354.2 3.2 fusion.23
  357.4 1.8 fusion.26
  359.3 5.9 %gather_fusion.1 = bf16[1024,1664]{1,0:T(8,128)(2,1)} fusion(bf16[1024,1664]{1,0:T(8,128)(2,1)S(1)} %fusion.26, s32[1024]{0:T(1024)S(1)} %broadcast_clamp_fusion), kind=kCustom, calls=%fused_computation.1 | custom fusion | bytes 6819840 | tf_op jit(solution)/shard_map/jit(_take)/gather | solution.py:111
  365.1 5.4 %gather.15 = bf16[256,6656]{1,0:T(8,128)(2,1)S(1)} reshape(bf16[1024,1664]{1,0:T(8,128)(2,1)} %gather_fusion.1) | data formatting | bytes 6815744 | tf_op jit(solution)/shard_map/jit(_take)/gather | solution.py:111
  370.6 33.4 %all-gather.10.cloned.1.call-done = bf16[6656,416]{1,0:T(8,128)(2,1)} async-done(((bf16[208,416]{1,0:T(8,128)(2,1)}), bf16[6656,416]{1,0:T(8,128)(2,1)}) %all-gather.10.cloned.1.call-update) | async-done | bytes 5537808 | tf_op jit(solution)/shard_map/all_gather | solution.py:117
  403.9 7.0 %convolution_convert_fusion.1 = bf16[512,416]{0,1:T(8,128)(2,1)} fusion(bf16[6656,416]{1,0:T(8,128)(2,1)} %all-gather.10.cloned.1.call-done, pred[256,6656]{1,0:T(8,128)(4,1)} %bitcast.122, bf16[256,6656]{1,0:T(8,128)(2,1)S(1)} %gather.15, s32[256]{0:T(256)S(1)} %multiply_add_fusion, f32[416]{0:T(512)S(1)} %copy-done.17), kind=kOutput, calls=%fused_computation.70 | convolution fusion | flops 1528987648 | bytes 11078272 | tf_op jit(solution)/shard_map/dot_general | solution.py:138
  410.9 1.2 copy.37
  412.1 16.2 %all_to_all.5 = bf16[32,16,416]{2,1,0:T(8,128)(2,1)S(1)} all-to-all(bf16[32,16,416]{2,1,0:T(8,128)(2,1)S(1)} %bitcast.120), channel_id=1, replica_groups=mesh['blk'=4,'tok'=32] {'tok'}, dimensions={0} | all-to-all | bytes 851968 | tf_op jit(solution)/shard_map/all_to_all | solution.py:140
  428.3 0.8 copy.63
  (71 shorter events, 1.0 us)
Async XLA Ops:
  6.5 71.2 %copy-start.1 = (bf16[1,256,1664]{2,1,0:T(8,128)(2,1)S(1)}, bf16[1,256,1664]{2,1,0:T(8,128)(2,1)}, u32[]{:S(2)}) copy-start(bf16[1,256,1664]{2,1,0:T(8,128)(2,1)} %param.22) | copy-start | bytes 2555908
  6.5 71.2 %copy-start.7 = (f32[1664]{0:T(1024)S(1)}, f32[1664]{0:T(1024)}, u32[]{:S(2)}) copy-start(f32[1664]{0:T(1024)} %param.26) | copy-start | bytes 19972
  6.5 71.2 %copy-start.6 = (f32[1664]{0:T(1024)S(1)}, f32[1664]{0:T(1024)}, u32[]{:S(2)}) copy-start(f32[1664]{0:T(1024)} %param.27) | copy-start | bytes 19972
  6.5 76.8 %all-gather.12.cloned.1.call-start = ((), (), s32[]{:S(2)}) async-start(), calls=%async_computation.7 | async-start | bytes 1892352 | tf_op jit(solution)/shard_map/all_gather | solution.py:84
  7.3 101.3 %all-gather.6.cloned.1.call-start = ((), (), s32[]{:S(2)}) async-start(), calls=%async_computation.2 | async-start | bytes 7028736 | tf_op jit(solution)/shard_map/all_gather | solution.py:57
  9.0 171.8 %reduce-scatter.2.cloned.1.call-start = ((), (), s32[]{:S(2)}) async-start(), calls=%async_computation.3 | async-start | bytes 4259840 | tf_op jit(solution)/shard_map/reduce_scatter | solution.py:85
  13.6 21.7 %collective-permute-start = (bf16[256,1664]{1,0:T(8,128)(2,1)S(1)}, bf16[256,1664]{1,0:T(8,128)(2,1)S(1)}, u32[]{:S(2)}, u32[]{:S(2)}) collective-permute-start(bf16[256,1664]{1,0:T(8,128)(2,1)S(1)} %fusion.47), channel_id=1, source_target_pairs={{0,32},{32,64},{64,96},{96,0},{1,33},{33,65},{65,97},{97,1},{2,34}... | collective-permute-start | bytes 2555912 | tf_op jit(solution)/shard_map/ppermute | solution.py:48
  35.3 20.1 %collective-permute-start.1 = (bf16[256,1664]{1,0:T(8,128)(2,1)S(1)}, bf16[256,1664]{1,0:T(8,128)(2,1)S(1)}, u32[]{:S(2)}, u32[]{:S(2)}) collective-permute-start(bf16[256,1664]{1,0:T(8,128)(2,1)S(1)} %collective-permute-done), channel_id=1, source_target_pairs={{0,32},{32,64},{64,96},{96,0},{1,33},{33,65},{65,97},{97,1},{2,34}... | collective-permute-start | bytes 2555912 | tf_op jit(solution)/shard_map/ppermute | solution.py:48
  55.4 19.3 %collective-permute-start.2 = (bf16[256,1664]{1,0:T(8,128)(2,1)S(1)}, bf16[256,1664]{1,0:T(8,128)(2,1)S(1)}, u32[]{:S(2)}, u32[]{:S(2)}) collective-permute-start(bf16[256,1664]{1,0:T(8,128)(2,1)S(1)} %collective-permute-done.1), channel_id=1, source_target_pairs={{0,32},{32,64},{64,96},{96,0},{1,33},{33,65},{65,97},{97,1},{2,34}... | collective-permute-start | bytes 2555912 | tf_op jit(solution)/shard_map/ppermute | solution.py:48
  76.7 31.9 %copy-start.15 = (f32[3,416]{1,0:T(4,128)S(1)}, f32[3,416]{1,0:T(4,128)}, u32[]{:S(2)}) copy-start(f32[3,416]{1,0:T(4,128)} %param.29) | copy-start | bytes 14980
  117.8 2.8 copy-start
  120.5 17.4 %copy-start.4 = (bf16[1664,416]{1,0:T(8,128)(2,1)S(1)}, bf16[1664,416]{1,0:T(8,128)(2,1)}, u32[]{:S(2)}) copy-start(bf16[1664,416]{1,0:T(8,128)(2,1)} %reshape.179) | copy-start | bytes 4153348
  138.0 42.9 %copy-start.5 = (f32[1664]{0:T(1024)S(1)}, f32[1664]{0:T(1024)}, u32[]{:S(2)}) copy-start(f32[1664]{0:T(1024)} %param.31) | copy-start | bytes 19972
  141.9 42.2 %copy-start.10 = (f32[1664]{0:T(1024)S(1)}, f32[1664]{0:T(1024)}, u32[]{:S(2)}) copy-start(f32[1664]{0:T(1024)} %param.33) | copy-start | bytes 19972
  141.9 42.2 %copy-start.11 = (f32[1664]{0:T(1024)S(1)}, f32[1664]{0:T(1024)}, u32[]{:S(2)}) copy-start(f32[1664]{0:T(1024)} %param.32) | copy-start | bytes 19972
  141.9 86.3 %all-gather.8.cloned.1.call-start = ((), (), s32[]{:S(2)}) async-start(), calls=%async_computation.4 | async-start | bytes 4259840 | tf_op jit(solution)/shard_map/all_gather | solution.py:95
  186.7 164.6 %all-reduce.2.cloned.1.call-start = ((), (), s32[]{:S(2)}) async-start(), calls=%async_computation.5 | async-start | bytes 6815744 | tf_op jit(solution)/shard_map/psum | solution.py:106
  186.8 52.8 %copy-start.16 = (f32[2048]{0:T(1024)S(1)}, f32[2048]{0:T(1024)}, u32[]{:S(2)}) copy-start(f32[2048]{0:T(1024)} %param.35) | copy-start | bytes 24580
  239.6 28.7 %copy-start.3 = (bf16[256,1664]{1,0:T(8,128)(2,1)S(1)}, bf16[256,1664]{1,0:T(8,128)(2,1)}, u32[]{:S(2)}) copy-start(bf16[256,1664]{1,0:T(8,128)(2,1)} %reduce-scatter.2.cloned.1.call-done) | copy-start | bytes 2555908
  268.7 2.8 copy-start.9
  268.8 4.5 %copy-start.14 = (s32[1,32]{1,0:T(1,128)S(1)}, s32[1,32]{1,0:T(1,128)}, u32[]{:S(2)}) copy-start(s32[1,32]{1,0:T(1,128)} %param.25) | copy-start | bytes 388
  270.9 80.4 %copy-start.8 = (f32[1664]{0:T(1024)S(1)}, f32[1664]{0:T(1024)}, u32[]{:S(2)}) copy-start(f32[1664]{0:T(1024)} %param.37) | copy-start | bytes 19972
  271.0 133.0 %all-gather.10.cloned.1.call-start = ((), (), s32[]{:S(2)}) async-start(), calls=%async_computation.6 | async-start | bytes 7028736 | tf_op jit(solution)/shard_map/all_gather | solution.py:117
  271.6 85.8 %copy-start.12 = (f32[1664]{0:T(1024)S(1)}, f32[1664]{0:T(1024)}, u32[]{:S(2)}) copy-start(f32[1664]{0:T(1024)} %param.39) | copy-start | bytes 19972
  271.6 85.8 %copy-start.13 = (f32[1664]{0:T(1024)S(1)}, f32[1664]{0:T(1024)}, u32[]{:S(2)}) copy-start(f32[1664]{0:T(1024)} %param.38) | copy-start | bytes 19972
  351.3 6.1 %copy-start.2 = (bf16[1024,1664]{1,0:T(8,128)(2,1)S(1)}, bf16[1024,1664]{1,0:T(8,128)(2,1)}, u32[]{:S(2)}) copy-start(bf16[1024,1664]{1,0:T(8,128)(2,1)} %all-reduce.2.cloned.1.call-done) | copy-start | bytes 10223620
  365.1 38.8 %copy-start.17 = (f32[416]{0:T(512)S(1)}, f32[416]{0:T(512)}, u32[]{:S(2)}) copy-start(f32[416]{0:T(512)} %param.41) | copy-start | bytes 4996
Sparse Core Ops, SparseCore 0:
  9.6 47.2 all-gather.11
  59.1 49.3 all-gather.5
  142.1 38.7 reduce-scatter.1
  186.8 41.3 all-gather.7
  271.1 80.1 all-reduce.1
  353.4 50.4 all-gather.9
